TPU v7x, 512 devices: a whole 4x4x16 slice. The times are simulated.
512 devices in a mesh: row: 16 (over z_lo, y), col: 32 (over x, z_hi, core).
Axes of the slice: x: 4, y: 4, z: 16 (z_hi: 4, z_lo: 4; z = z_hi * 4 + z_lo), core: 2. Of those that a mesh axis runs over, the one named last changes fastest.
Arguments:
- tiles: bfloat16 [16, 32, 32, 128, 128], P('row', 'col'), may hold values from -0.5 to 0.5
- tile_slots: int32 [16, 32, 32], P('row', 'col'), may hold values from 0 to 191, as said below
- tile_counts: int32 [16, 32], P('row', 'col'), may hold values from 8 to 32, as said below
- user_degree: int32 [32768], P('row'), may hold values from 1 to 64
- item_degree: int32 [49152], P('col'), may hold values from 1 to 64
- start_panel: float32 [64, 49152], P(None, ('col', 'row')), may hold values from -6 to 6
Outputs:
- left_panel: float32 [64, 32768], P(None, ('row', 'col'))
- right_panel: float32 [64, 49152], P(None, ('col', 'row'))
- left_factors: float32 [3, 64, 64], replicated
- right_factors: float32 [3, 64, 64], replicated
Inputs may be any that keep to these rules, and one draw needn't show every extreme that they name: `tile_slots`: within one grid cell the 32 slot numbers are distinct; slot s is local tile row s // 12 and local tile column s % 12; entries from position tile_counts on are padding. `tile_counts`: some grid cell holds 32 live tiles.
All inputs are finite; a program needn't handle non-finite values.
Results may differ from a plain program's by a relative error of at most 0.0005.
Values sent between devices are 32-bit elements; how exact they have to be, the bound alone decides.
No kernel may reach another device: no remote copies, remote signals or barrier semaphores. Data moves between devices by JAX's collectives and lax.ppermute only.
A program may use at most 64 MiB of HBM per device.

v0:
```python
import math
import jax
import jax.numpy as jnp
from jax import lax
from jax.sharding import PartitionSpec as P

STEPS = 3
HIGH = lax.Precision.HIGHEST


def gram_of(vectors):
    return jnp.einsum("bn,cn->bc", vectors, vectors, precision=HIGH)


def solve_lower(factor, vectors):
    return lax.linalg.triangular_solve(factor, vectors, left_side=True, lower=True)


def per_device(tiles, tile_slots, tile_counts, user_degree, item_degree, start_panel):
    tile_stack = tiles[0, 0].astype(jnp.float32)
    slot_list = tile_slots[0, 0]
    tile_total = tile_counts[0, 0]
    slot_count = tile_stack.shape[0]
    tile_width = tile_stack.shape[1]
    row_blocks = user_degree.shape[0] // tile_width
    col_blocks = item_degree.shape[0] // tile_width
    block_width = start_panel.shape[0]
    live_mask = jnp.arange(slot_count) < tile_total
    local_rows = slot_list // col_blocks
    local_cols = slot_list % col_blocks
    row_select = (
        (local_rows[:, None] == jnp.arange(row_blocks)[None, :]) & live_mask[:, None]
    ).astype(jnp.float32)
    col_select = (
        (local_cols[:, None] == jnp.arange(col_blocks)[None, :]) & live_mask[:, None]
    ).astype(jnp.float32)
    user_scale = lax.rsqrt(user_degree.astype(jnp.float32))
    item_scale = lax.rsqrt(item_degree.astype(jnp.float32))
    user_group = row_blocks * tile_width // lax.axis_size("col")
    item_group = col_blocks * tile_width // lax.axis_size("row")
    user_offset = lax.axis_index("col") * user_group
    item_offset = lax.axis_index("row") * item_group
    user_scale_own = lax.dynamic_slice_in_dim(user_scale, user_offset, user_group)
    item_scale_own = lax.dynamic_slice_in_dim(item_scale, item_offset, item_group)
    start_total = lax.psum(gram_of(start_panel), ("row", "col"))
    start_factor = jnp.linalg.cholesky(start_total)
    item_basis = solve_lower(start_factor, start_panel)
    user_basis = start_panel[:, :0]
    item_factor = start_factor
    user_list = []
    item_list = []
    for iteration in range(STEPS):
        scaled = item_basis * item_scale_own[None, :]
        item_full = lax.all_gather(scaled, "row", axis=1, tiled=True)
        forward_panel_blocks = item_full.reshape(block_width, col_blocks, tile_width)
        forward_chosen = jnp.take(forward_panel_blocks, local_cols, axis=1)
        forward_partial_value = jnp.einsum(
            "mrc,bmc->bmr", tile_stack, forward_chosen, precision=HIGH
        )
        forward_summed = jnp.einsum(
            "bmr,mk->bkr", forward_partial_value, row_select, precision=HIGH
        )
        forward = (
            lax.psum_scatter(
                forward_summed.reshape(block_width, row_blocks * tile_width),
                "col",
                scatter_dimension=1,
                tiled=True,
            )
            * user_scale_own[None, :]
        )
        if iteration > 0:
            forward = forward - jnp.dot(item_factor.T, user_basis, precision=HIGH)
        user_factor = jnp.linalg.cholesky(lax.psum(gram_of(forward), ("row", "col")))
        user_basis = solve_lower(user_factor, forward)
        scaled = user_basis * user_scale_own[None, :]
        user_full = lax.all_gather(scaled, "col", axis=1, tiled=True)
        panel_blocks = user_full.reshape(block_width, row_blocks, tile_width)
        chosen = jnp.take(panel_blocks, local_rows, axis=1)
        partial_value = jnp.einsum("mrc,bmr->bmc", tile_stack, chosen, precision=HIGH)
        summed = jnp.einsum("bmc,mk->bkc", partial_value, col_select, precision=HIGH)
        backward = (
            lax.psum_scatter(
                summed.reshape(block_width, col_blocks * tile_width),
                "row",
                scatter_dimension=1,
                tiled=True,
            )
            * item_scale_own[None, :]
        )
        backward = backward - jnp.dot(user_factor.T, item_basis, precision=HIGH)
        item_factor = jnp.linalg.cholesky(lax.psum(gram_of(backward), ("row", "col")))
        item_basis = solve_lower(item_factor, backward)
        user_list.append(user_factor)
        item_list.append(item_factor)
    user_total = row_blocks * tile_width * lax.axis_size("row")
    item_total = col_blocks * tile_width * lax.axis_size("col")
    return (
        math.sqrt(user_total) * user_basis,
        math.sqrt(item_total) * item_basis,
        jnp.stack(user_list),
        jnp.stack(item_list),
    )


def solution(mesh):
    in_specs = (
        P("row", "col", None, None, None),
        P("row", "col", None),
        P("row", "col"),
        P("row"),
        P("col"),
        P(None, ("col", "row")),
    )
    out_specs = (P(None, ("row", "col")), P(None, ("col", "row")), P(), P())
    return jax.shard_map(
        per_device, mesh=mesh, in_specs=in_specs, out_specs=out_specs, check_vma=False
    )
```

profile of v0, /device:TPU:1, one launch (start us, length us, event | category | flops | bytes accessed | tf_op | source)
XLA Modules:
  0.0 1727.9 jit_solution(9248479124465914468)
XLA Ops:
  9.7 111.2 %psum.49 = f32[64,64]{0,1:T(8,128)S(1)} all-reduce(f32[64,64]{0,1:T(8,128)S(1)} %fusion.153), channel_id=1, replica_groups=mesh['row'=16,'col'=32] {'row','col'}, use_global_device_ids=true, to_apply=%region_0.1 | all-reduce | flops 4096 | bytes 32768 | tf_op jit(solution)/shard_map/psum | solution.py:45
  120.9 5.8 cholesky.119
  128.1 4.9 custom-call.13
  134.1 33.8 %all-gather = f32[16,96,64]{1,2,0:T(8,128)S(1)} all-gather(f32[1,96,64]{1,2,0:T(8,128)S(1)} %multiply_bitcast_fusion.2), channel_id=1, replica_groups=mesh['row'=16,'col'=32] {'row'}, dimensions={0}, use_global_device_ids=true | all-gather | bytes 417792 | tf_op jit(solution)/shard_map/all_gather | solution.py:54
  174.6 110.4 %reduce-scatter.19.cloned.1.call-done = f32[64,64]{1,0:T(8,128)} async-done(((f32[2048,64]{1,0:T(8,128)}), f32[64,64]{1,0:T(8,128)}) %reduce-scatter.19.cloned.1.call-update) | async-done | bytes 16400
  286.0 101.8 %psum.50 = f32[64,64]{0,1:T(8,128)S(1)} all-reduce(f32[64,64]{0,1:T(8,128)S(1)} %fusion.81), channel_id=1, replica_groups=mesh['row'=16,'col'=32] {'row','col'}, use_global_device_ids=true, to_apply=%region_4.8 | all-reduce | flops 4096 | bytes 32768 | tf_op jit(solution)/shard_map/psum | solution.py:74
  388.0 5.8 cholesky.130
  395.1 4.9 custom-call.14
  400.4 57.0 %all_gather.19 = f32[64,2048]{0,1:T(8,128)S(1)} all-gather(f32[64,64]{0,1:T(8,128)S(1)} %copy.109), channel_id=1, replica_groups=mesh['row'=16,'col'=32] {'col'}, dimensions={1}, use_global_device_ids=true | all-gather | bytes 540672 | tf_op jit(solution)/shard_map/all_gather | solution.py:77
  461.6 71.2 %reduce-scatter.21.cloned.1.call-done = f32[96,64]{1,0:T(8,128)} async-done(((f32[1536,64]{1,0:T(8,128)}), f32[96,64]{1,0:T(8,128)}) %reduce-scatter.21.cloned.1.call-update) | async-done | bytes 24592
  534.8 112.8 %psum.51 = f32[64,64]{0,1:T(8,128)S(1)} all-reduce(f32[64,64]{0,1:T(8,128)S(1)} %fusion.154), channel_id=1, replica_groups=mesh['row'=16,'col'=32] {'row','col'}, use_global_device_ids=true, to_apply=%region_6.12 | all-reduce | flops 4096 | bytes 32768 | tf_op jit(solution)/shard_map/psum | solution.py:92
  647.7 5.8 cholesky.141
  654.9 4.9 custom-call.15
  660.0 36.4 %all-gather.1 = f32[16,96,64]{1,2,0:T(8,128)S(1)} all-gather(f32[1,96,64]{1,2,0:T(8,128)S(1)} %multiply_bitcast_fusion.1), channel_id=1, replica_groups=mesh['row'=16,'col'=32] {'row'}, dimensions={0}, use_global_device_ids=true | all-gather | bytes 417792 | tf_op jit(solution)/shard_map/all_gather | solution.py:54
  702.3 110.1 %reduce-scatter.23.cloned.1.call-done = f32[64,64]{1,0:T(8,128)} async-done(((f32[2048,64]{1,0:T(8,128)}), f32[64,64]{1,0:T(8,128)}) %reduce-scatter.23.cloned.1.call-update) | async-done | bytes 16400
  814.3 102.0 %psum.52 = f32[64,64]{0,1:T(8,128)S(1)} all-reduce(f32[64,64]{0,1:T(8,128)S(1)} %fusion.155), channel_id=1, replica_groups=mesh['row'=16,'col'=32] {'row','col'}, use_global_device_ids=true, to_apply=%region_8.14 | all-reduce | flops 4096 | bytes 32768 | tf_op jit(solution)/shard_map/psum | solution.py:74
  916.4 5.8 cholesky.152
  923.6 4.9 custom-call.16
  928.9 56.4 %all_gather.21 = f32[64,2048]{0,1:T(8,128)S(1)} all-gather(f32[64,64]{0,1:T(8,128)S(1)} %copy.120), channel_id=1, replica_groups=mesh['row'=16,'col'=32] {'col'}, dimensions={1}, use_global_device_ids=true | all-gather | bytes 540672 | tf_op jit(solution)/shard_map/all_gather | solution.py:77
  989.6 70.9 %reduce-scatter.25.cloned.1.call-done = f32[96,64]{1,0:T(8,128)} async-done(((f32[1536,64]{1,0:T(8,128)}), f32[96,64]{1,0:T(8,128)}) %reduce-scatter.25.cloned.1.call-update) | async-done | bytes 24592
  1062.5 113.1 %psum.53 = f32[64,64]{0,1:T(8,128)S(1)} all-reduce(f32[64,64]{0,1:T(8,128)S(1)} %fusion.156), channel_id=1, replica_groups=mesh['row'=16,'col'=32] {'row','col'}, use_global_device_ids=true, to_apply=%region_10.16 | all-reduce | flops 4096 | bytes 32768 | tf_op jit(solution)/shard_map/psum | solution.py:92
  1175.6 5.8 cholesky.163
  1182.8 4.9 custom-call.17
  1188.0 36.7 %all-gather.2 = f32[16,96,64]{1,2,0:T(8,128)S(1)} all-gather(f32[1,96,64]{1,2,0:T(8,128)S(1)} %multiply_bitcast_fusion), channel_id=1, replica_groups=mesh['row'=16,'col'=32] {'row'}, dimensions={0}, use_global_device_ids=true | all-gather | bytes 417792 | tf_op jit(solution)/shard_map/all_gather | solution.py:54
  1230.5 110.1 %reduce-scatter.27.cloned.1.call-done = f32[64,64]{1,0:T(8,128)} async-done(((f32[2048,64]{1,0:T(8,128)}), f32[64,64]{1,0:T(8,128)}) %reduce-scatter.27.cloned.1.call-update) | async-done | bytes 16400
  1342.5 101.8 %psum.54 = f32[64,64]{0,1:T(8,128)S(1)} all-reduce(f32[64,64]{0,1:T(8,128)S(1)} %fusion.157), channel_id=1, replica_groups=mesh['row'=16,'col'=32] {'row','col'}, use_global_device_ids=true, to_apply=%region_12.18 | all-reduce | flops 4096 | bytes 32768 | tf_op jit(solution)/shard_map/psum | solution.py:74
  1444.4 5.8 cholesky.174
  1451.6 4.9 custom-call.18
  1457.5 56.3 %all_gather.23 = f32[64,2048]{0,1:T(8,128)S(1)} all-gather(f32[64,64]{0,1:T(8,128)S(1)} %copy.131), channel_id=1, replica_groups=mesh['row'=16,'col'=32] {'col'}, dimensions={1}, use_global_device_ids=true | all-gather | bytes 540672 | tf_op jit(solution)/shard_map/all_gather | solution.py:77
  1518.7 73.4 %reduce-scatter.29.cloned.1.call-done = f32[96,64]{1,0:T(8,128)} async-done(((f32[1536,64]{1,0:T(8,128)}), f32[96,64]{1,0:T(8,128)}) %reduce-scatter.29.cloned.1.call-update) | async-done | bytes 24592
  1594.0 113.0 %psum.55 = f32[64,64]{0,1:T(8,128)S(1)} all-reduce(f32[64,64]{0,1:T(8,128)S(1)} %fusion.158), channel_id=1, replica_groups=mesh['row'=16,'col'=32] {'row','col'}, use_global_device_ids=true, to_apply=%region_14.20 | all-reduce | flops 4096 | bytes 32768 | tf_op jit(solution)/shard_map/psum | solution.py:92
  1707.1 5.8 cholesky.185
  (130 shorter events, 63.5 us)
Async XLA Ops:
  7.2 161.9 %copy-start = (bf16[1,1,32,128,128]{4,3,2,1,0:T(8,128)(2,1)S(1)}, bf16[1,1,32,128,128]{4,3,2,1,0:T(8,128)(2,1)}, u32[]{:S(2)}) copy-start(bf16[1,1,32,128,128]{4,3,2,1,0:T(8,128)(2,1)} %param.15) | copy-start | bytes 3145732
  7.2 277.8 %reduce-scatter.19.cloned.1.call-start = ((), (), s32[]{:S(2)}) async-start(), calls=%async_computation.6 | async-start | bytes 1081344
  8.0 0.7 copy-start.2
  127.5 5.6 copy-start.1
  173.7 359.1 %reduce-scatter.21.cloned.1.call-start = ((), (), s32[]{:S(2)}) async-start(), calls=%async_computation.7 | async-start | bytes 835584
  461.6 350.8 %reduce-scatter.23.cloned.1.call-start = ((), (), s32[]{:S(2)}) async-start(), calls=%async_computation.8 | async-start | bytes 1081344
  702.3 358.2 %reduce-scatter.25.cloned.1.call-start = ((), (), s32[]{:S(2)}) async-start(), calls=%async_computation.9 | async-start | bytes 835584
  989.5 351.1 %reduce-scatter.27.cloned.1.call-start = ((), (), s32[]{:S(2)}) async-start(), calls=%async_computation.10 | async-start | bytes 1081344
  1230.5 361.6 %reduce-scatter.29.cloned.1.call-start = ((), (), s32[]{:S(2)}) async-start(), calls=%async_computation.11 | async-start | bytes 835584
Sparse Core Ops, SparseCore 0:
  173.9 111.0 reduce-scatter.18
  461.7 71.0 reduce-scatter.20
  702.4 109.9 reduce-scatter.22
  989.6 70.8 reduce-scatter.24
  1230.6 109.9 reduce-scatter.26
  1518.1 73.8 reduce-scatter.28
where the time goes:
time: 1740 us; the launch traced here: 1730 us
  blocking collectives  1030 us (59%)
  waiting for transfers between devices  546 us (31%)
  other arithmetic  87.5 us (5%)
  matrix products  25.6 us (1%)
  local copies, waits for them, and re-layouts  20.4 us (1%)
    unnamed x12, waiting for transfers between devices  546 us
    psum x3, blocking collectives, per_device(): lax.psum(gram_of(backward), ('row', 'col'))  339 us
    psum x3, blocking collectives, per_device(): lax.psum(gram_of(forward), ('row', 'col'))  306 us
    all_gather x3, blocking collectives, per_device(): user_full = lax.all_gather(scaled, 'col', axis=1, tiled=True)  170 us
    psum x1, blocking collectives, per_device(): start_total = lax.psum(gram_of(start_panel), ('row', 'col'))  111 us
    all_gather x3, blocking collectives, per_device(): item_full = lax.all_gather(scaled, 'row', axis=1, tiled=True)  107 us
    another operation x8, other arithmetic, solve_lower(): lax.linalg.triangular_solve(factor, vectors, left_side=True, lower=True)  34.9 us
  transfers between devices with their start and end apart: 6, of which 6 were waited for; matrix products, arithmetic and copies ran while one was open for 0% of the time, Pallas kernels for 0%

commit v1 on v0

--- a/solution.py
+++ b/solution.py
@@ -6,6 +6,14 @@
 
 STEPS = 3
 HIGH = lax.Precision.HIGHEST
+
+
+def shape_keys(local, peer_axis, dim_no):
+    g_now = lax.axis_size(peer_axis)
+    tmp = jnp.stack([local] * g_now, axis=0)
+    front = lax.all_to_all(tmp, peer_axis, 0, 0)
+    earlier = jnp.concatenate(front, axis=dim_no)
+    return earlier
 
 
 def gram_of(vectors):
@@ -51,7 +59,7 @@
     item_list = []
     for iteration in range(STEPS):
         scaled = item_basis * item_scale_own[None, :]
-        item_full = lax.all_gather(scaled, "row", axis=1, tiled=True)
+        item_full = shape_keys(scaled, "row", 1)
         forward_panel_blocks = item_full.reshape(block_width, col_blocks, tile_width)
         forward_chosen = jnp.take(forward_panel_blocks, local_cols, axis=1)
         forward_partial_value = jnp.einsum(

time: 1740 us -> 1670 us (0.960)
  blocking collectives: 1030 us -> 965 us
    all_gather x3 -> x0, blocking collectives: 107 us -> none  [per_device(): item_full = lax.all_gather(scaled, 'row', axis=1, tiled=True)]
    all_to_all x0 -> x2, blocking collectives: none -> 38 us  [shape_keys(): front = lax.all_to_all(tmp, peer_axis, 0, 0)]
  transfers between devices with their start and end apart: 6 -> 7, of which waited for: 6 -> 7; matrix products, arithmetic and copies ran while one was open for 0% -> 0% of each run, Pallas kernels for 0% -> 0%
where the time goes in v1:
time: 1670 us; the launch traced here: 1660 us
  blocking collectives  965 us (58%)
  waiting for transfers between devices  541 us (32%)
  other arithmetic  87.5 us (5%)
  matrix products  25.6 us (2%)
  local copies, waits for them, and re-layouts  21.4 us (1%)
    unnamed x12, waiting for transfers between devices  529 us
    psum x3, blocking collectives, per_device(): lax.psum(gram_of(backward), ('row', 'col'))  339 us
    psum x3, blocking collectives, per_device(): lax.psum(gram_of(forward), ('row', 'col'))  306 us
    all_gather x3, blocking collectives, per_device(): user_full = lax.all_gather(scaled, 'col', axis=1, tiled=True)  171 us
    psum x1, blocking collectives, per_device(): start_total = lax.psum(gram_of(start_panel), ('row', 'col'))  111 us
    all_to_all x2, blocking collectives, shape_keys(): front = lax.all_to_all(tmp, peer_axis, 0, 0)  38 us
    another operation x8, other arithmetic, solve_lower(): lax.linalg.triangular_solve(factor, vectors, left_side=True, lower=True)  34.9 us
  transfers between devices with their start and end apart: 7, of which 7 were waited for; matrix products, arithmetic and copies ran while one was open for 0% of the time, Pallas kernels for 0%

profile of v1, /device:TPU:1, one launch (start us, length us, event | category | flops | bytes accessed | tf_op | source)
XLA Modules:
  0.0 1660.6 jit_solution(11717541913926504305)
XLA Ops:
  8.2 111.2 %psum.49 = f32[64,64]{0,1:T(8,128)S(1)} all-reduce(f32[64,64]{0,1:T(8,128)S(1)} %fusion.153), channel_id=1, replica_groups=mesh['row'=16,'col'=32] {'row','col'}, use_global_device_ids=true, to_apply=%region_0.1 | all-reduce | flops 4096 | bytes 32768 | tf_op jit(solution)/shard_map/psum | solution.py:53
  119.5 5.8 cholesky.119
  126.7 4.9 custom-call.13
  138.4 12.4 all-to-all-done
  157.6 105.9 %reduce-scatter.19.cloned.1.call-done = f32[64,64]{1,0:T(8,128)} async-done(((f32[2048,64]{1,0:T(8,128)}), f32[64,64]{1,0:T(8,128)}) %reduce-scatter.19.cloned.1.call-update) | async-done | bytes 16400
  264.6 101.8 %psum.50 = f32[64,64]{0,1:T(8,128)S(1)} all-reduce(f32[64,64]{0,1:T(8,128)S(1)} %fusion.81), channel_id=1, replica_groups=mesh['row'=16,'col'=32] {'row','col'}, use_global_device_ids=true, to_apply=%region_4.8 | all-reduce | flops 4096 | bytes 32768 | tf_op jit(solution)/shard_map/psum | solution.py:82
  366.5 5.8 cholesky.130
  373.7 4.9 custom-call.14
  378.9 57.9 %all_gather.9 = f32[64,2048]{0,1:T(8,128)S(1)} all-gather(f32[64,64]{0,1:T(8,128)S(1)} %copy.80), channel_id=1, replica_groups=mesh['row'=16,'col'=32] {'col'}, dimensions={1}, use_global_device_ids=true | all-gather | bytes 540672 | tf_op jit(solution)/shard_map/all_gather | solution.py:85
  441.1 71.8 %reduce-scatter.21.cloned.1.call-done = f32[96,64]{1,0:T(8,128)} async-done(((f32[1536,64]{1,0:T(8,128)}), f32[96,64]{1,0:T(8,128)}) %reduce-scatter.21.cloned.1.call-update) | async-done | bytes 24592
  514.9 113.1 %psum.51 = f32[64,64]{0,1:T(8,128)S(1)} all-reduce(f32[64,64]{0,1:T(8,128)S(1)} %fusion.154), channel_id=1, replica_groups=mesh['row'=16,'col'=32] {'row','col'}, use_global_device_ids=true, to_apply=%region_6.12 | all-reduce | flops 4096 | bytes 32768 | tf_op jit(solution)/shard_map/psum | solution.py:100
  628.1 5.8 cholesky.141
  635.3 4.9 custom-call.15
  640.5 18.9 %all_to_all.15 = f32[16,64,96]{2,1,0:T(8,128)S(1)} all-to-all(f32[16,64,96]{2,1,0:T(8,128)S(1)} %stack.23), channel_id=1, replica_groups=mesh['row'=16,'col'=32] {'row'}, dimensions={0} | all-to-all | bytes 786432 | tf_op jit(solution)/shard_map/all_to_all | solution.py:14
  665.3 105.9 %reduce-scatter.23.cloned.1.call-done = f32[64,64]{1,0:T(8,128)} async-done(((f32[2048,64]{1,0:T(8,128)}), f32[64,64]{1,0:T(8,128)}) %reduce-scatter.23.cloned.1.call-update) | async-done | bytes 16400
  773.1 102.0 %psum.52 = f32[64,64]{0,1:T(8,128)S(1)} all-reduce(f32[64,64]{0,1:T(8,128)S(1)} %fusion.155), channel_id=1, replica_groups=mesh['row'=16,'col'=32] {'row','col'}, use_global_device_ids=true, to_apply=%region_8.14 | all-reduce | flops 4096 | bytes 32768 | tf_op jit(solution)/shard_map/psum | solution.py:82
  875.2 5.8 cholesky.152
  882.4 4.9 custom-call.16
  887.6 56.8 %all_gather.10 = f32[64,2048]{0,1:T(8,128)S(1)} all-gather(f32[64,64]{0,1:T(8,128)S(1)} %copy.91), channel_id=1, replica_groups=mesh['row'=16,'col'=32] {'col'}, dimensions={1}, use_global_device_ids=true | all-gather | bytes 540672 | tf_op jit(solution)/shard_map/all_gather | solution.py:85
  948.7 69.1 %reduce-scatter.25.cloned.1.call-done = f32[96,64]{1,0:T(8,128)} async-done(((f32[1536,64]{1,0:T(8,128)}), f32[96,64]{1,0:T(8,128)}) %reduce-scatter.25.cloned.1.call-update) | async-done | bytes 24592
  1019.8 113.2 %psum.53 = f32[64,64]{0,1:T(8,128)S(1)} all-reduce(f32[64,64]{0,1:T(8,128)S(1)} %fusion.156), channel_id=1, replica_groups=mesh['row'=16,'col'=32] {'row','col'}, use_global_device_ids=true, to_apply=%region_10.16 | all-reduce | flops 4096 | bytes 32768 | tf_op jit(solution)/shard_map/psum | solution.py:100
  1133.1 5.8 cholesky.163
  1140.3 4.9 custom-call.17
  1145.5 19.1 %all_to_all.16 = f32[16,64,96]{2,1,0:T(8,128)S(1)} all-to-all(f32[16,64,96]{2,1,0:T(8,128)S(1)} %stack.24), channel_id=1, replica_groups=mesh['row'=16,'col'=32] {'row'}, dimensions={0} | all-to-all | bytes 786432 | tf_op jit(solution)/shard_map/all_to_all | solution.py:14
  1170.5 105.9 %reduce-scatter.27.cloned.1.call-done = f32[64,64]{1,0:T(8,128)} async-done(((f32[2048,64]{1,0:T(8,128)}), f32[64,64]{1,0:T(8,128)}) %reduce-scatter.27.cloned.1.call-update) | async-done | bytes 16400
  1278.3 101.8 %psum.54 = f32[64,64]{0,1:T(8,128)S(1)} all-reduce(f32[64,64]{0,1:T(8,128)S(1)} %fusion.157), channel_id=1, replica_groups=mesh['row'=16,'col'=32] {'row','col'}, use_global_device_ids=true, to_apply=%region_12.18 | all-reduce | flops 4096 | bytes 32768 | tf_op jit(solution)/shard_map/psum | solution.py:82
  1380.3 5.8 cholesky.174
  1387.5 4.9 custom-call.18
  1393.3 56.3 %all_gather.11 = f32[64,2048]{0,1:T(8,128)S(1)} all-gather(f32[64,64]{0,1:T(8,128)S(1)} %copy.102), channel_id=1, replica_groups=mesh['row'=16,'col'=32] {'col'}, dimensions={1}, use_global_device_ids=true | all-gather | bytes 540672 | tf_op jit(solution)/shard_map/all_gather | solution.py:85
  1454.5 70.3 %reduce-scatter.29.cloned.1.call-done = f32[96,64]{1,0:T(8,128)} async-done(((f32[1536,64]{1,0:T(8,128)}), f32[96,64]{1,0:T(8,128)}) %reduce-scatter.29.cloned.1.call-update) | async-done | bytes 24592
  1526.7 113.1 %psum.55 = f32[64,64]{0,1:T(8,128)S(1)} all-reduce(f32[64,64]{0,1:T(8,128)S(1)} %fusion.158), channel_id=1, replica_groups=mesh['row'=16,'col'=32] {'row','col'}, use_global_device_ids=true, to_apply=%region_14.20 | all-reduce | flops 4096 | bytes 32768 | tf_op jit(solution)/shard_map/psum | solution.py:100
  1639.9 5.8 cholesky.185
  (131 shorter events, 68.1 us)
Async XLA Ops:
  7.2 145.0 %copy-start = (bf16[1,1,32,128,128]{4,3,2,1,0:T(8,128)(2,1)S(1)}, bf16[1,1,32,128,128]{4,3,2,1,0:T(8,128)(2,1)}, u32[]{:S(2)}) copy-start(bf16[1,1,32,128,128]{4,3,2,1,0:T(8,128)(2,1)} %param.15) | copy-start | bytes 3145732
  126.0 6.4 copy-start.1
  133.5 17.4 %all-to-all-start = ((f32[16,64,96]{2,1,0:T(8,128)}), f32[16,64,96]{2,1,0:T(8,128)S(1)}, u32[]{:S(2)}, u32[]{:S(2)}) async-start(f32[16,64,96]{2,1,0:T(8,128)} %stack.22), calls=%async_computation | async-start | bytes 1048576 | tf_op jit(solution)/shard_map/all_to_all | solution.py:14
  137.0 126.5 %reduce-scatter.19.cloned.1.call-start = ((), (), s32[]{:S(2)}) async-start(), calls=%async_computation.9 | async-start | bytes 1081344
  137.7 0.7 copy-start.2
  156.8 356.2 %reduce-scatter.21.cloned.1.call-start = ((), (), s32[]{:S(2)}) async-start(), calls=%async_computation.10 | async-start | bytes 835584
  441.1 330.1 %reduce-scatter.23.cloned.1.call-start = ((), (), s32[]{:S(2)}) async-start(), calls=%async_computation.11 | async-start | bytes 1081344
  665.3 352.6 %reduce-scatter.25.cloned.1.call-start = ((), (), s32[]{:S(2)}) async-start(), calls=%async_computation.12 | async-start | bytes 835584
  948.7 327.7 %reduce-scatter.27.cloned.1.call-start = ((), (), s32[]{:S(2)}) async-start(), calls=%async_computation.13 | async-start | bytes 1081344
  1170.5 354.3 %reduce-scatter.29.cloned.1.call-start = ((), (), s32[]{:S(2)}) async-start(), calls=%async_computation.14 | async-start | bytes 835584
Sparse Core Ops, SparseCore 0:
  156.9 106.6 reduce-scatter.18
  441.2 71.6 reduce-scatter.20
  665.4 105.7 reduce-scatter.22
  948.8 69.0 reduce-scatter.24
  1170.6 105.8 reduce-scatter.26
  1453.9 70.7 reduce-scatter.28
